TPU v7x, 32 devices: a whole 2x2x4 slice. The times are simulated.
32 devices in a mesh: rows: 8 (over z, y), heads: 4 (over x, core).
Axes of the slice: x: 2, y: 2, z: 4, core: 2. Of those that a mesh axis runs over, the one named last changes fastest.
Arguments:
- hidden_in: bfloat16 [64, 512, 768], P('rows', 'heads'), may hold values from -6 to 6
- lengths: int32 [64, 4], P('rows'), may hold values from 1 to 256, 512 in all within a row
- qkv_weight: bfloat16 [768, 2304], replicated, may hold values from -0.21875 to 0.21875
- query_bias: bfloat16 [768], replicated, may hold values from -3 to 3
- value_bias: bfloat16 [768], replicated, may hold values from -0.59765625 to 0.59765625
- out_weight: bfloat16 [768, 768], replicated, may hold values from -1.75 to 1.75
- out_bias: bfloat16 [768], replicated, may hold values from -1.1953125 to 1.1953125
- gain_one: bfloat16 [768], replicated, may hold values from 0.5 to 1.5
- shift_one: bfloat16 [768], replicated, may hold values from -1.1953125 to 1.1953125
- up_weight: bfloat16 [768, 3072], replicated, may hold values from -0.21875 to 0.21875
- up_bias: bfloat16 [3072], replicated, may hold values from -1.1953125 to 1.1953125
- down_weight: bfloat16 [3072, 768], replicated, may hold values from -0.15625 to 0.15625
- down_bias: bfloat16 [768], replicated, may hold values from -1.1953125 to 1.1953125
- gain_two: bfloat16 [768], replicated, may hold values from 0.5 to 1.5
- shift_two: bfloat16 [768], replicated, may hold values from -1.1953125 to 1.1953125
- cotangent: bfloat16 [64, 512, 768], P('rows', 'heads'), may hold values from -6 to 6
Outputs:
- layer_out: bfloat16 [64, 512, 768], P('rows', 'heads')
- input_grad: float32 [64, 512, 768], P('rows', 'heads')
- qkv_grad: float32 [768, 2304], P('rows', 'heads')
- querybias_grad: float32 [768], replicated
- valuebias_grad: float32 [768], replicated
- outweight_grad: float32 [768, 768], P('rows', 'heads')
- outbias_grad: float32 [768], replicated
- gainone_grad: float32 [768], replicated
- shiftone_grad: float32 [768], replicated
- upweight_grad: float32 [768, 3072], P('rows', 'heads')
- upbias_grad: float32 [3072], replicated
- downweight_grad: float32 [3072, 768], P('rows', 'heads')
- downbias_grad: float32 [768], replicated
- gaintwo_grad: float32 [768], replicated
- shifttwo_grad: float32 [768], replicated
Inputs may be any that keep to these rules, and one draw needn't show every extreme that they name: The 4 lengths of a packed row sum to 512; in every row the longest is 256.
All inputs are finite; a program needn't handle non-finite values.
Results may differ from a plain program's by a relative error of at most 0.017.
Values may be sent and summed in bfloat16 or wider, within the bound.
A program may use at most 192 MiB of HBM per device.

v0:
```python
import functools

import jax
import jax.numpy as jnp
from jax import lax
from jax.experimental import pallas as pl
from jax.experimental.pallas import tpu as pltpu
from jax.sharding import PartitionSpec as P

DH = 64
D = 768
L = 512
EPSILON = 1e-12
OFF = -(2.0**100)
F32 = jnp.float32
BF16 = jnp.bfloat16
NN = (((1,), (0,)), ((), ()))
NT = (((1,), (1,)), ((), ()))
TN = (((0,), (0,)), ((), ()))

RATE = 0.285
TAIL = (
    0.11576503423350087,
    0.08983941546025678,
    0.2103671707394457,
    -0.14882089196252246,
    0.3285619517018635,
    -0.09571266010718714,
)


def mm(left, right, dims=NN):
    return lax.dot_general(left, right, dims, preferred_element_type=F32)


def normal_parts(u):
    bell = jnp.exp2(u * u * -0.7213475204444817)
    t = pltpu.reciprocal(1.0 + RATE * jnp.abs(u))
    poly = TAIL[-1]
    for item in TAIL[-2::-1]:
        poly = poly * t + item
    tail = poly * t * bell
    return jnp.where(u >= 0, 1.0 - tail, tail), bell * 0.3989422804014327


def norm_parts(values):
    middle = jnp.mean(values, axis=-1, keepdims=True)
    center = values - middle
    spread = jnp.mean(center * center, axis=-1, keepdims=True)
    scale = lax.rsqrt(spread + EPSILON)
    return center * scale, scale


def norm_back(grad, normed, scale, gain):
    dn = grad * gain
    first = jnp.mean(dn, axis=-1, keepdims=True)
    second = jnp.mean(dn * normed, axis=-1, keepdims=True)
    return (dn - first - normed * second) * scale


def split3(values):
    high = values.astype(BF16)
    rest = values - high.astype(F32)
    mid = rest.astype(BF16)
    return high, mid, (rest - mid.astype(F32)).astype(BF16)


def features(ends, key_feat, query_feat, start):
    token = lax.broadcasted_iota(jnp.int32, (L, 128), 0)
    place = lax.broadcasted_iota(jnp.int32, (L, 128), 1) & (DH - 1)
    seg = jnp.zeros((L, 128), jnp.int32)
    for end in ends:
        seg = seg + (token >= end).astype(jnp.int32)
    count = len(ends)
    ones = (place == seg) | ((place >= count) & (place < count + 3))
    key_feat[pl.ds(start, L), :] = jnp.where(ones, 1.0, 0.0).astype(BF16)
    off = (place < count) & (place != seg)
    query_feat[pl.ds(start, L), :] = jnp.where(off, OFF, 0.0).astype(BF16)


def attend(rows, group, pairs, qkv, ctx, lse, key_feat, query_feat):
    lane = lax.broadcasted_iota(jnp.int32, (1, 128), 1)
    kf, qf = key_feat[rows, :], query_feat[rows, :]
    ops, values = [], []
    for pair in range(pairs):
        col = pl.multiple_of(group * (pairs * 128) + pair * 128, 128)
        q2 = qkv[rows, pl.ds(col, 128)]
        k2 = qkv[rows, pl.ds(D + col, 128)]
        values.append(qkv[rows, pl.ds(2 * D + col, 128)])
        for own in (lane < DH, lane >= DH):
            ops.append((jnp.where(own, q2, qf), jnp.where(own, k2, kf)))
    count = 2 * pairs
    scores = [None] * count
    outs, sums = [], []
    scores[0] = mm(*ops[0], NT)
    for head in range(count):
        if head + 1 < count:
            scores[head + 1] = mm(*ops[head + 1], NT)
        peak = jnp.max(scores[head], axis=1, keepdims=True)
        expo = jnp.exp(scores[head] - peak)
        total = jnp.sum(expo, axis=1, keepdims=True)
        out = mm(expo.astype(BF16), values[head // 2])
        outs.append(out * (1.0 / total))
        sums.append(peak + jnp.log(total))
    keep = jnp.zeros((L, 128), F32)
    for head in range(count):
        keep = jnp.where(lane == head, sums[head], keep)
    lse[group, rows, :] = keep
    for pair in range(pairs):
        col = pl.multiple_of(group * (pairs * 128) + pair * 128, 128)
        both = jnp.where(lane < DH, outs[2 * pair], outs[2 * pair + 1])
        ctx[rows, pl.ds(col, 128)] = both.astype(BF16)


def attend_back(rows, group, pairs, qkv, ctx, dctx, keep, grads, kf, qf):
    lane = lax.broadcasted_iota(jnp.int32, (1, 128), 1)
    place = lane & (DH - 1)
    vf = jnp.where((place >= 4) & (place < 7), 1.0, 0.0).astype(BF16)

    def spread(column, base):
        high, mid, small = split3(-column)
        return jnp.where(
            place == 4, high, jnp.where(place == 5, mid, jnp.where(place == 6, small, base))
        )

    ops = []
    for pair in range(pairs):
        col = pl.multiple_of(group * (pairs * 128) + pair * 128, 128)
        q2 = qkv[rows, pl.ds(col, 128)]
        k2 = qkv[rows, pl.ds(D + col, 128)]
        v2 = qkv[rows, pl.ds(2 * D + col, 128)]
        d2 = dctx[rows, pl.ds(col, 128)]
        both = d2.astype(F32) * ctx[rows, pl.ds(col, 128)].astype(F32)
        zero = jnp.zeros_like(q2)
        for side, own in enumerate((lane < DH, lane >= DH)):
            inner = jnp.sum(jnp.where(own, both, 0.0), axis=1, keepdims=True)
            total = keep[:, 2 * pair + side : 2 * pair + side + 1]
            ops.append(
                (
                    jnp.where(own, k2, kf),
                    jnp.where(own, q2, spread(total, qf)),
                    jnp.where(own, v2, vf),
                    jnp.where(own, d2, spread(inner, zero)),
                    jnp.where(own, q2, zero),
                    jnp.where(own, k2, zero),
                    jnp.where(own, d2, zero),
                )
            )
    count = 2 * pairs
    scores, chances = [None] * count, [None] * count
    dq, dk, dv = [0] * pairs, [0] * pairs, [0] * pairs

    def start(head):
        scores[head] = mm(ops[head][0], ops[head][1], NT)
        chances[head] = mm(ops[head][2], ops[head][3], NT)

    start(0)
    for head in range(count):
        if head + 1 < count:
            start(head + 1)
        chance = jnp.exp(scores[head])
        low = chance.astype(BF16)
        ds = (chance * chances[head]).astype(BF16)
        pair = head // 2
        dk[pair] += mm(ds, ops[head][4])
        dv[pair] += mm(low, ops[head][6])
        dq[pair] += mm(ds, ops[head][5], TN)
    for pair in range(pairs):
        col = pl.multiple_of(group * (pairs * 128) + pair * 128, 128)
        grads[rows, pl.ds(col, 128)] = (dq[pair] * DH**-0.5).astype(BF16)
        grads[rows, pl.ds(D + col, 128)] = dk[pair].astype(BF16)
        grads[rows, pl.ds(2 * D + col, 128)] = dv[pair].astype(BF16)


def first_kernel(x, lens, wqkv, bqkv, wout, bout, qkv, ctx, r1, lse, key_feat, query_feat):
    for row in range(x.shape[0] // L):
        ends, total = [], 0
        for item in range(lens.shape[1]):
            total = total + lens[row, item]
            ends.append(total)
        features(ends, key_feat, query_feat, row * L)

        rows = pl.ds(row * L, L)
        for part in range(3):
            cols = pl.ds(part * D, D)
            acc = mm(x[rows, :], wqkv[:, cols]) + bqkv[:, cols]
            if part == 0:
                acc = acc * DH**-0.5
            qkv[rows, cols] = acc.astype(BF16)

        def heads(group, carry):
            attend(rows, group, 3, qkv, ctx, lse, key_feat, query_feat)
            return carry

        lax.fori_loop(0, 2, heads, 0)
        r1[rows, :] = mm(ctx[rows, :], wout[...]) + bout[...] + x[rows, :].astype(F32)


def middle_kernel(
    r1, ctx, cot, vecs, wup, bup, wdown, wout,
    y, dr1, dctx, downg, upg, outg, vec_grads, upb_grad,
    fb, act, slope, acc, dfb, dab,
):
    tokens = r1.shape[0]
    step = 256
    parts = tokens // step
    width = 768
    chunks = wup.shape[1] // width
    g1, s1, g2, s2, bd = (vecs[i : i + 1, :] for i in range(5))
    vec_grads[...] = jnp.zeros_like(vec_grads)
    upb_grad[...] = jnp.zeros_like(upb_grad)

    def lead(i, carry):
        rows = pl.ds(pl.multiple_of(i * step, step), step)
        normed, _ = norm_parts(r1[rows, :])
        first = normed * g1 + s1
        fb[rows, :] = first.astype(BF16)
        acc[rows, :] = first + bd
        return carry

    lax.fori_loop(0, parts, lead, 0)

    def forward(c, carry):
        cols = pl.ds(pl.multiple_of(c * width, width), width)
        u, e = [None] * parts, [None] * parts
        for s in range(parts + 2):
            if s < parts:
                u[s] = mm(fb[s * step : (s + 1) * step, :], wup[:, cols]) + bup[:, cols]
            if 0 <= s - 1 < parts:
                j = s - 1
                rows = slice(j * step, (j + 1) * step)
                cdf, pdf = normal_parts(u[j])
                e[j] = (u[j] * cdf).astype(BF16)
                act[rows, cols] = e[j]
                slope[rows, cols] = (cdf + u[j] * pdf).astype(BF16)
            if 0 <= s - 2 < parts:
                j = s - 2
                acc[j * step : (j + 1) * step, :] += mm(e[j], wdown[cols, :])
        return carry

    lax.fori_loop(0, chunks, forward, 0)

    def second(i, carry):
        rows = pl.ds(pl.multiple_of(i * step, step), step)
        normed, scale = norm_parts(acc[rows, :])
        y[rows, :] = (normed * g2 + s2).astype(BF16)
        dy = cot[rows, :].astype(F32)
        dr2 = norm_back(dy, normed, scale, g2)
        acc[rows, :] = dr2
        low = dr2.astype(BF16)
        dfb[rows, :] = low
        vec_grads[0:1, :] += jnp.sum(dy * normed, axis=0, keepdims=True)
        vec_grads[1:2, :] += jnp.sum(dy, axis=0, keepdims=True)
        vec_grads[2:3, :] += jnp.sum(low.astype(F32), axis=0, keepdims=True)
        return carry

    lax.fori_loop(0, parts, second, 0)

    def down(c, carry):
        cols = pl.ds(pl.multiple_of(c * width, width), width)
        downg[:, cols] = mm(dfb[...], act[:, cols], TN).astype(BF16)
        return carry

    lax.fori_loop(0, chunks, down, 0)

    def backward(c, carry):
        cols = pl.ds(pl.multiple_of(c * width, width), width)
        de, du = [None] * parts, [None] * parts
        sums = jnp.zeros((1, width), F32)
        for s in range(parts + 2):
            if s < parts:
                de[s] = mm(dfb[s * step : (s + 1) * step, :], wdown[cols, :], NT)
            if 0 <= s - 1 < parts:
                j = s - 1
                rows = slice(j * step, (j + 1) * step)
                du[j] = (de[j] * slope[rows, cols].astype(F32)).astype(BF16)
                slope[rows, cols] = du[j]
                sums = sums + jnp.sum(du[j].astype(F32), axis=0, keepdims=True)
            if 0 <= s - 2 < parts:
                j = s - 2
                acc[j * step : (j + 1) * step, :] += mm(du[j], wup[:, cols], NT)
        upb_grad[:, cols] = sums
        return carry

    lax.fori_loop(0, chunks, backward, 0)

    def third(i, carry):
        rows = pl.ds(pl.multiple_of(i * step, step), step)
        normed, scale = norm_parts(r1[rows, :])
        grad = acc[rows, :]
        dr = norm_back(grad, normed, scale, g1)
        dr1[rows, :] = dr
        low = dr.astype(BF16)
        dab[rows, :] = low
        vec_grads[3:4, :] += jnp.sum(grad * normed, axis=0, keepdims=True)
        vec_grads[4:5, :] += jnp.sum(grad, axis=0, keepdims=True)
        vec_grads[5:6, :] += jnp.sum(low.astype(F32), axis=0, keepdims=True)
        return carry

    lax.fori_loop(0, parts, third, 0)
    dctx[...] = mm(dab[...], wout[...], NT).astype(BF16)
    outg[...] = mm(ctx[...], dab[...], TN).astype(BF16)

    def up(c, carry):
        cols = pl.ds(pl.multiple_of(c * width, width), width)
        upg[:, cols] = mm(fb[...], slope[:, cols], TN).astype(BF16)
        return carry

    lax.fori_loop(0, chunks, up, 0)


def last_kernel(x, lens, qkv, ctx, dctx, lse, dr1, wqkv, xg, qkvg, vec_grads, grads, key_feat, query_feat):
    vec_grads[...] = jnp.zeros_like(vec_grads)
    for row in range(x.shape[0] // L):
        ends, total = [], 0
        for item in range(lens.shape[1]):
            total = total + lens[row, item]
            ends.append(total)
        features(ends, key_feat, query_feat, row * L)

        rows = pl.ds(row * L, L)

        def heads(group, carry):
            attend_back(
                rows, group, 3, qkv, ctx, dctx, lse[group, rows, :], grads, key_feat[rows, :], query_feat[rows, :]
            )
            return carry

        lax.fori_loop(0, 2, heads, 0)
    vec_grads[0:1, :] = jnp.sum(grads[:, 0:D].astype(F32), axis=0, keepdims=True)
    vec_grads[1:2, :] = jnp.sum(grads[:, 2 * D : 3 * D].astype(F32), axis=0, keepdims=True)
    for part in range(3):
        cols = slice(part * D, (part + 1) * D)
        qkvg[:, cols] = mm(x[...], grads[:, cols], TN).astype(BF16)
    xg[...] = (mm(grads[...], wqkv[...], NT) + dr1[...]).astype(xg.dtype)


MESH = pl.DeviceIdType.MESH


def load(source, target, sem):
    copy = pltpu.make_async_copy(source, target, sem)
    copy.start()
    return copy


def remote(source, target, out_sem, in_sem, device):
    return pltpu.make_async_remote_copy(
        src_ref=source, dst_ref=target, send_sem=out_sem, recv_sem=in_sem,
        device_id=device, device_id_type=MESH,
    )


def arrived(target, in_sem, device):
    remote(target, target, in_sem, in_sem, device).wait_recv()


def meet(devices):
    barrier = pltpu.get_barrier_semaphore()
    for device in devices:
        pl.semaphore_signal(barrier, inc=1, device_id=device, device_id_type=MESH)
    pl.semaphore_wait(barrier, len(devices))


def example_ends(lens, row):
    place = lax.broadcasted_iota(jnp.int32, lens.shape, 1)
    counts = jnp.sum(jnp.where(place == row, lens[...], 0).astype(F32), axis=1, keepdims=True)
    ends, total = [], 0
    for item in range(lens.shape[0]):
        total = total + counts[item : item + 1, :]
        ends.append(total.astype(jnp.int32))
    return ends


def wide(vector):
    return vector[...].astype(F32).reshape(1, vector.shape[0])


def gather_kernel(
    hidden, lens, wqkv_in, bq, bv, wout_in, bout,
    x_out, qkv_out, ctx_out, r1_out, lse_out,
    x, qkv, ctx, r1, lse, wqkv, wout, bias, key_feat, query_feat,
    load_sem, own_sem, keep_sem, out_sems, in_sems,
):
    me = lax.axis_index("heads")
    row_id = lax.axis_index("rows")
    heads = lax.axis_size("heads")
    part = hidden.shape[1]
    rows_mine = x.shape[0] // L
    wqkv_load = load(wqkv_in, wqkv, load_sem.at[0])
    wout_load = load(wout_in, wout, load_sem.at[1])
    others = [lax.rem(me + step, heads) for step in range(1, heads)]
    device = lambda other: {"rows": row_id, "heads": other}

    def kept(row):
        return pltpu.make_async_copy(
            hidden.at[me * rows_mine + row], x.at[pl.ds(row * L + me * part, part)], own_sem.at[row]
        )

    def passed(row, step):
        other = others[step]
        return remote(
            hidden.at[other * rows_mine + row], x.at[pl.ds(row * L + me * part, part)],
            out_sems.at[row, step], in_sems.at[row, me], device(other),
        )

    def stores(row):
        rows = pl.ds(pl.multiple_of(row * L, L), L)
        return [
            pltpu.make_async_copy(source, target, keep_sem.at[index, row])
            for index, (source, target) in enumerate(
                (
                    (x.at[rows], x_out.at[rows]), (qkv.at[rows], qkv_out.at[rows]), (ctx.at[rows], ctx_out.at[rows]),
                    (lse.at[:, rows], lse_out.at[:, rows]), (r1.at[rows], r1_out.at[rows]),
                )
            )
        ]

    meet([device(other) for other in others])
    for row in range(rows_mine):
        for step in range(heads - 1):
            passed(row, step).start()
        kept(row).start()
    bias[0:1, :] = wide(bq)
    bias[1:2, :] = jnp.zeros((1, D), F32)
    bias[2:3, :] = wide(bv)
    out_bias = wide(bout)
    for row in range(rows_mine):
        features(example_ends(lens, me * rows_mine + row), key_feat, query_feat, row * L)
    wqkv_load.wait()
    side, sibling = me // 2, me + 1 - 2 * lax.rem(me, 2)
    near = L // (heads // 2)

    def project(row, half):
        rows = pl.ds(pl.multiple_of(row * L + half * near, near), near)
        for item in range(3):
            cols = pl.ds(item * D, D)
            acc = mm(x[rows, :], wqkv[:, cols]) + bias[item : item + 1, :]
            if item == 0:
                acc = acc * DH**-0.5
            qkv[rows, cols] = acc.astype(BF16)

    def take(row, other):
        arrived(x.at[pl.ds(row * L + other * part, part)], in_sems.at[row, other], device(other))

    def this_chip(row, carry):
        kept(row).wait()
        take(row, sibling)
        project(row, side)
        return carry

    lax.fori_loop(0, rows_mine, this_chip, 0)
    wout_load.wait()

    def whole_row(row, carry):
        rows = pl.ds(pl.multiple_of(row * L, L), L)
        for item in range(heads - 2):
            take(row, lax.rem(2 * side + 2 + item, heads))
        keep = stores(row)
        keep[0].start()
        project(row, 1 - side)
        keep[1].start()

        def group_heads(group, carry):
            attend(rows, group, 3, qkv, ctx, lse, key_feat, query_feat)
            return carry

        lax.fori_loop(0, 2, group_heads, 0)
        keep[2].start()
        keep[3].start()
        r1[rows, :] = mm(ctx[rows, :], wout[...]) + out_bias + x[rows, :].astype(F32)
        keep[4].start()
        return carry

    lax.fori_loop(0, rows_mine, whole_row, 0)
    for row in range(rows_mine):
        for step in range(heads - 1):
            passed(row, step).wait_send()
        for copy in stores(row):
            copy.wait()


class Place:
    def __init__(self):
        self.row, self.head = lax.axis_index("rows"), lax.axis_index("heads")
        self.z, self.y = self.row // 2, lax.rem(self.row, 2)
        self.x, self.c = self.head // 2, lax.rem(self.head, 2)
        self.half, self.low = self.z // 2, lax.rem(self.z, 2)
        self.next_z = self.at(z=2 * self.half + 1 - self.low)
        self.far_z = self.at(z=2 * (1 - self.half) + self.low)
        self.cross_z = self.at(z=2 * (1 - self.half) + 1 - self.low)
        self.over = {
            "c": self.at(c=1 - self.c), "y": self.at(y=1 - self.y), "x": self.at(x=1 - self.x),
        }

    def at(self, **new):
        z, y, x, c = (new.get(name, getattr(self, name)) for name in "zyxc")
        return {"rows": z * 2 + y, "heads": x * 2 + c}

    def turn(self, step):
        first, second = lax.rem(step, 2), step // 2
        half = self.half + (1 - first) * (1 - 2 * self.half)
        low = self.low + (1 - second) * (1 - 2 * self.low)
        return 2 * half + low

    def side(self, name):
        return self.y if name == "y" else self.x


class Total:
    def __init__(self, where, order, got, mid, far, near, sems, apart=False):
        self.where, self.order, self.direct = where, order.lower(), "Z" in order
        self.got, self.mid, self.far, self.near = got, mid, far, near
        self.core_out, self.core_in, self.out, self.inn, self.z_in = sems
        self.apart = apart

    @staticmethod
    def scratch(order, rows, cols, pieces, groups=()):
        shapes = [(2, 4, 2, rows, cols), (2, 4, rows, cols), (4, rows, cols), (4, rows, cols)]
        stages = 2
        if order[0] == "y":
            shapes[2:] = [(4, 2, rows, cols), (rows, cols)]
            stages = 1
        sems = [(pieces,) if pieces > 2 else (1,), (pieces,), (stages + 2,), (stages, 4), (4,)]
        spaces = [pltpu.VMEM(groups + dims, BF16) for dims in shapes]
        return spaces + [pltpu.SemaphoreType.DMA(groups + dims) for dims in sems]

    def core_copy(self, index, parts):
        source, target = parts(index)
        out = self.core_out.at[index if self.apart else 0]
        return remote(source, target, out, self.core_in.at[index], self.where.over["c"])

    def core_sent(self):
        remote(self.got, self.got, self.core_out.at[0], self.core_in.at[0], self.where.over["c"]).wait_send()

    def core_wait(self, index, target):
        arrived(target, self.core_in.at[index], self.where.over["c"])

    def part(self, ref, z, side):
        return ref.at[side, z] if self.order[0] == "x" else ref.at[:, z, side]

    def first_copy(self, step):
        w = self.where
        z = w.turn(step)
        source = self.part(self.got, z, 1 - w.side(self.order[0]))
        return remote(source, self.mid.at[:, z], self.out.at[0], self.inn.at[0, step], w.over[self.order[0]])

    def first(self, step):
        self.first_copy(step).start()

    def second_copy(self, step):
        w = self.where
        z = w.turn(step)
        source = self.mid.at[1 - w.side(self.order[1]), z]
        return remote(source, self.far.at[z], self.out.at[2], self.inn.at[1, step], w.over[self.order[1]])

    def second(self, step):
        w = self.where
        z = w.turn(step)
        arrived(self.mid.at[:, z], self.inn.at[0, step], w.over[self.order[0]])
        own = self.part(self.got, z, w.side(self.order[0]))
        self.mid[:, z] = (self.mid[:, z].astype(F32) + own[...].astype(F32)).astype(BF16)
        if self.order == "yzx":
            self.z_send(step)
        else:
            self.second_copy(step).start()

    def third(self, step):
        if self.order == "yzx":
            return
        w = self.where
        z = w.turn(step)
        arrived(self.far.at[z], self.inn.at[1, step], w.over[self.order[1]])
        own = self.mid[w.side(self.order[1]), z]
        self.far[z] = (self.far[z].astype(F32) + own.astype(F32)).astype(BF16)
        self.z_send(step)

    def z_slots(self):
        return self.far if self.order == "yzx" else self.near

    def z_block(self, step):
        z = self.where.turn(step)
        return self.mid.at[:, z] if self.order == "yzx" else self.far.at[z]

    def z_device(self, step):
        w = self.where
        return w.next_z if step == 1 else w.far_z if step == 2 else w.cross_z if self.direct else w.next_z

    def z_copy(self, step):
        return remote(
            self.z_block(step), self.z_slots().at[step], self.out.at[1], self.z_in.at[step], self.z_device(step)
        )

    def z_take(self, step):
        arrived(self.z_slots().at[step], self.z_in.at[step], self.z_device(step))
        return self.z_slots()[step].astype(F32)

    def z_send(self, step):
        if step < (3 if self.direct else 2):
            self.z_copy(step).start()

    def relay(self):
        if self.direct:
            return
        block = self.z_block(2)
        block[...] = (block[...].astype(F32) + self.z_take(0)).astype(BF16)
        self.z_copy(2).start()

    def z_sum(self):
        total = self.z_block(3)[...].astype(F32) + self.z_take(1) + self.z_take(2)
        return total + self.z_take(0) if self.direct else total

    def x_copy(self):
        w = self.where
        return remote(self.far.at[3, 1 - w.x], self.near, self.out.at[2], self.z_in.at[3], w.over["x"])

    def fourth(self):
        if self.order != "yzx":
            return
        self.far[3] = self.z_sum().astype(BF16)
        self.x_copy().start()

    def result(self):
        w = self.where
        if self.order != "yzx":
            return self.z_sum()
        arrived(self.near, self.z_in.at[3], w.over["x"])
        return self.far[3, w.x].astype(F32) + self.near[...].astype(F32)

    def sent(self):
        w = self.where
        remote(self.mid, self.mid, self.out.at[0], self.inn.at[0, 0], w.over["y"]).wait_send()
        blocks = self.z_slots().at[pl.ds(0, 3)]
        remote(blocks, blocks, self.out.at[1], self.z_in.at[0], w.next_z).wait_send()
        if self.order == "yzx":
            self.x_copy().wait_send()
        else:
            remote(self.far, self.far, self.out.at[2], self.inn.at[1, 0], w.over["y"]).wait_send()


class Everyone:
    def __init__(self, where, by_head, by_row, sems):
        self.where, self.by_head, self.by_row, self.sems = where, by_head, by_row, sems
        self.own = by_head.at[where.head]

    @staticmethod
    def scratch(rows):
        return [pltpu.VMEM((4, rows, D), F32), pltpu.VMEM((8, rows, D), F32), pltpu.SemaphoreType.DMA((14,))]

    def head_copy(self, step):
        w = self.where
        return remote(
            self.own, self.own, self.sems.at[0], self.sems.at[2 + w.head],
            {"rows": w.row, "heads": lax.rem(w.head + step, 4)},
        )

    def row_copy(self, step):
        w = self.where
        mine = self.by_row.at[w.row]
        return remote(
            mine, mine, self.sems.at[1], self.sems.at[6 + w.row],
            {"rows": lax.rem(w.row + step, 8), "heads": w.head},
        )

    def start(self):
        for step in range(1, 4):
            self.head_copy(step).start()

    def middle(self):
        w = self.where
        for step in range(1, 4):
            head = lax.rem(w.head + step, 4)
            arrived(self.by_head.at[head], self.sems.at[2 + head], {"rows": w.row, "heads": head})
        self.by_row[w.row] = (self.by_head[0] + self.by_head[1]) + (self.by_head[2] + self.by_head[3])
        for step in range(1, 8):
            self.row_copy(step).start()

    def result(self):
        w = self.where
        for step in range(1, 8):
            row = lax.rem(w.row + step, 8)
            arrived(self.by_row.at[row], self.sems.at[6 + row], {"rows": row, "heads": w.head})
        total = self.by_row[0]
        for row in range(1, 8):
            total = total + self.by_row[row]
        return total

    def sent(self):
        w = self.where
        for ref, count, sem in ((self.by_head, 3, 0), (self.by_row, 7, 1)):
            part = ref.at[pl.ds(0, count)]
            remote(part, part, self.sems.at[sem], self.sems.at[2], w.over["y"]).wait_send()


def rest_kernel(
    scale,
    r1_in, cotan, ctx_in, qkv_in, lse_in, x_in, lens, wup_in, wdown_in, wout_in, wqkv_in,
    g1v, s1v, g2v, s2v, bdv, bup,
    lay, xgr, down_to, up_to, out_to, qkv_to, vec_to,
    downo, upo, outo, qkvo, vec_out, mat_sem, r1, ycot, fb, act, slope, acc, dfb, dfbt, wup, wdown, down_send,
    load_sem, cot_sem, lay_sem, xg_sem, own_sem,
    *scratch,
):
    where = w = Place()
    scratch = list(scratch)

    def take(count):
        return [scratch.pop(0) for _ in range(count)]

    totals = []
    for order, *_ in BLOCKS:
        refs = take(9)
        totals.append(Total(where, order, *refs[:4], refs[4:], apart=not totals))
    down, upa, upb, out = totals
    joint = [(order, take(9)) for order, *_ in JOINT]

    def qkv_pair(group):
        made = []
        for order, refs in joint:
            refs = [ref.at[group] for ref in refs]
            made.append(Total(where, order, *refs[:4], refs[4:]))
        return made

    qkvs = (qkv_pair(0), qkv_pair(1))
    everyone = Everyone(where, *take(3))
    late = Everyone(where, *take(3))

    tokens = r1.shape[0]
    step_rows = 256
    parts = tokens // step_rows
    width = 768
    chunks = wup_in.shape[1] // width
    rows_mine = tokens // L
    part = lay.shape[1]
    r1_rows = [pl.ds(index * step_rows, step_rows) for index in range(parts)]
    r1_loads = [load(r1_in.at[rows], r1.at[rows], load_sem.at[9 + index]) for index, rows in enumerate(r1_rows)]
    wup_load = load(wup_in, wup, load_sem.at[1])
    wdown_load = load(wdown_in, wdown, load_sem.at[2])
    others = [lax.rem(w.head + step, 4) for step in range(1, 4)]
    partner = lambda other: {"rows": w.row, "heads": other}
    g1, s1, g2, s2, bd = (wide(item) for item in (g1v, s1v, g2v, s2v, bdv))
    mine = everyone.own
    mine[...] = jnp.zeros(mine.shape, F32)
    last = late.own
    last[...] = jnp.zeros(last.shape, F32)

    def lead(i, carry):
        rows = pl.ds(pl.multiple_of(i * step_rows, step_rows), step_rows)
        pltpu.make_async_copy(r1_in.at[rows], r1.at[rows], load_sem.at[9 + i]).wait()
        normed, _ = norm_parts(r1[rows, :])
        first = normed * g1 + s1
        fb[rows, :] = first.astype(BF16)
        acc[rows, :] = first + bd
        return carry

    lax.fori_loop(0, parts, lead, 0)
    meet([partner(other) for other in others] + [{"rows": lax.rem(w.row + step, 8), "heads": w.head} for step in range(1, 8)])

    def mine_in(row):
        place = pl.ds(row * L + w.head * part, part)
        return pltpu.make_async_copy(cotan.at[w.head * rows_mine + row], ycot.at[place], own_sem.at[2, row])

    def cot_copy(row, step):
        place = pl.ds(row * L + w.head * part, part)
        other = others[step]
        return remote(
            cotan.at[other * rows_mine + row], ycot.at[place], cot_sem.at[0], cot_sem.at[1 + row],
            partner(other),
        )

    def give_back(source, target, sems, row, step):
        other = others[step]
        return remote(
            source.at[pl.ds(row * L + other * part, part)], target.at[w.head * rows_mine + row],
            sems.at[0], sems.at[1 + row], partner(other),
        )

    def mine_out(source, target, index, row):
        place = pl.ds(row * L + w.head * part, part)
        return pltpu.make_async_copy(source.at[place], target.at[w.head * rows_mine + row], own_sem.at[index, row])

    for row in range(rows_mine):
        for step in range(3):
            cot_copy(row, step).start()
        mine_in(row).start()

    wup_load.wait()
    wdown_load.wait()

    def forward(c, carry):
        cols = pl.ds(pl.multiple_of(c * width, width), width)
        u, e = [None] * parts, [None] * parts
        for s in range(parts + 2):
            if s < parts:
                u[s] = mm(fb[s * step_rows : (s + 1) * step_rows, :], wup[:, cols]) + wide(bup.at[cols])
            if 0 <= s - 1 < parts:
                j = s - 1
                rows = slice(j * step_rows, (j + 1) * step_rows)
                cdf, pdf = normal_parts(u[j])
                e[j] = (u[j] * cdf).astype(BF16)
                act[rows, cols] = e[j]
                slope[rows, cols] = (cdf + u[j] * pdf).astype(BF16)
            if 0 <= s - 2 < parts:
                j = s - 2
                acc[j * step_rows : (j + 1) * step_rows, :] += mm(e[j], wdown[cols, :])
        return carry

    lax.fori_loop(0, chunks, forward, 0)
    for row in range(rows_mine):
        mine_in(row).wait()
        arrived(ycot.at[pl.ds(row * L, 3 * part)], cot_sem.at[1 + row], partner(others[0]))

    def second(i, carry):
        rows = pl.ds(pl.multiple_of(i * step_rows, step_rows), step_rows)
        normed, spread = norm_parts(acc[rows, :])
        dy = ycot[rows, :].astype(F32)
        ycot[rows, :] = (normed * g2 + s2).astype(BF16)
        dr2 = norm_back(dy, normed, spread, g2)
        acc[rows, :] = dr2
        low = dr2.astype(BF16)
        dfb[rows, :] = low
        dfbt[:, :, rows] = low.T.reshape(4, D // 4, step_rows)
        mine[0:1, :] += jnp.sum(dy * normed, axis=0, keepdims=True)
        mine[1:2, :] += jnp.sum(dy, axis=0, keepdims=True)
        mine[2:3, :] += jnp.sum(low.astype(F32), axis=0, keepdims=True)
        return carry

    lax.fori_loop(0, parts, second, 0)

    for row in range(rows_mine):
        for step in range(3):
            give_back(ycot, lay, lay_sem, row, step).start()
        mine_out(ycot, lay, 0, row).start()

    def down_half(core, z):
        left = jnp.concatenate([dfbt[core], dfbt[2 + core]], axis=0)
        cols = pl.ds(pl.multiple_of(z * width, width), width)
        return mm(left, act[:, cols])

    quarter, eighth = D // 4, width // 2

    def down_parts(step):
        z = where.turn(step)
        return down_send.at[lax.rem(step, 2)], down.got.at[:, z]

    def down_other(step, carry):
        z = where.turn(step)
        total = down_half(1 - w.c, z)

        @pl.when(step >= 2)
        def _():
            down.core_copy(step - 2, down_parts).wait_send()

        slot = lax.rem(step, 2)
        for x in range(2):
            for y in range(2):
                piece = total[x * quarter : (x + 1) * quarter, y * eighth : (y + 1) * eighth]
                down_send[slot, x, y] = piece.astype(BF16)
        down.core_copy(step, down_parts).start()
        return carry

    def down_own(step, carry):
        z = where.turn(step)
        total = down_half(w.c, z)
        down.core_wait(step, down.got.at[:, z])
        for x in range(2):
            for y in range(2):
                piece = total[x * quarter : (x + 1) * quarter, y * eighth : (y + 1) * eighth]
                down.got[x, z, y] = (piece + down.got[x, z, y].astype(F32)).astype(BF16)
        down.first(step)
        return carry

    lax.fori_loop(0, 4, down_other, 0)
    lax.fori_loop(0, 4, down_own, 0)
    qkv_load = load(qkv_in, act.at[:, pl.ds(0, 3 * D)], load_sem.at[4])

    def backward(c, carry):
        cols = pl.ds(pl.multiple_of(c * width, width), width)
        de, du = [None] * parts, [None] * parts
        sums = jnp.zeros((1, width), F32)
        for s in range(parts + 2):
            if s < parts:
                de[s] = mm(dfb[s * step_rows : (s + 1) * step_rows, :], wdown[cols, :], NT)
            if 0 <= s - 1 < parts:
                j = s - 1
                rows = slice(j * step_rows, (j + 1) * step_rows)
                du[j] = (de[j] * slope[rows, cols].astype(F32)).astype(BF16)
                slope[rows, cols] = du[j]
                sums = sums + jnp.sum(du[j].astype(F32), axis=0, keepdims=True)
            if 0 <= s - 2 < parts:
                j = s - 2
                acc[j * step_rows : (j + 1) * step_rows, :] += mm(du[j], wup[:, cols], NT)
        mine[pl.ds(3 + c, 1), :] = sums
        return carry

    half = chunks // 2
    lax.fori_loop(0, half, backward, 0)
    down.second(0)
    lax.fori_loop(half, chunks, backward, 0)
    down.second(1)
    down.third(0)
    wqkv = wup.at[:, pl.ds(0, 3 * D)]
    x = wdown.at[pl.ds(2 * D, tokens)]
    wout = wup.at[:, pl.ds(3 * D, D)]
    wqkv_load = load(wqkv_in, wqkv, load_sem.at[5])
    wout_load = load(wout_in, wout, load_sem.at[3])
    x_load = load(x_in, x, load_sem.at[6])
    dab = dfb
    feats = wdown.at[pl.ds(2 * D + tokens, L)]
    for row in range(rows_mine):
        key_feat, query_feat = (feats.at[:, pl.ds((2 * row + item) * 128, 128)] for item in range(2))
        features(example_ends(lens, w.head * rows_mine + row), key_feat, query_feat, 0)

    def third(i, carry):
        rows = pl.ds(pl.multiple_of(i * step_rows, step_rows), step_rows)
        normed, spread = norm_parts(r1[rows, :])
        grad = acc[rows, :]
        dr = norm_back(grad, normed, spread, g1)
        acc[rows, :] = dr
        low = dr.astype(BF16)
        dab[rows, :] = low
        mine[7:8, :] += jnp.sum(grad * normed, axis=0, keepdims=True)
        last[2:3, :] += jnp.sum(grad, axis=0, keepdims=True)
        last[3:4, :] += jnp.sum(low.astype(F32), axis=0, keepdims=True)
        return carry

    lax.fori_loop(0, parts, third, 0)
    lse_load = [load(lse_in.at[g], r1.at[:, pl.ds(g * 128, 128)], load_sem.at[7 + g]) for g in range(2)]

    def up_half(core, x_side):
        cols = pl.ds(pl.multiple_of((2 * x_side + core) * width, width), width)
        return mm(fb[...], slope[:, cols], TN)

    ups = (upa, upb)

    def spot(side, index, cols, start):
        row = pl.multiple_of(side * D + index * (D // 2), D // 2)
        return wdown.at[pl.ds(row, D // 2), pl.ds(start, cols)]

    def pair_parts(each, index, cols, start):
        return lambda side: (spot(side, index, cols, start), each.got.at[side].reshape(D // 2, cols))

    def pair_other(pair, side, total, cols, start):
        total = total.astype(BF16).reshape(4, 2, 2, D // 16, cols)
        for index, each in enumerate(pair):
            spot(side, index, cols, start)[...] = total[:, :, index].reshape(D // 2, cols)
            each.core_copy(side, pair_parts(each, index, cols, start)).start()

    def pair_own(pair, side, turn, total, cols):
        total = total.reshape(4, 2, 2, D // 16, cols)
        for index, each in enumerate(pair):
            each.core_wait(side, each.got.at[side])
            each.got[side] = (total[:, :, index] + each.got[side].astype(F32)).astype(BF16)
        for when, each in enumerate((pair[1], pair[0])):

            @pl.when(turn == when)
            def _():
                for step in range(4):
                    each.first(step)

    def pair_sent(pair):
        for each in pair:
            each.core_sent()

    def far_first(turn):
        return lax.rem(w.x + 1 + turn, 2)

    def up_other(turn, carry):
        side = far_first(turn)
        pair_other(ups, side, up_half(1 - w.c, side), width, 0)
        return carry

    lax.fori_loop(0, 2, up_other, 0)
    down.second(2)
    down.relay()
    down.third(1)

    def up_own(turn, carry):
        side = far_first(turn)
        pair_own(ups, side, turn, up_half(w.c, side), width)
        return carry

    lax.fori_loop(0, 2, up_own, 0)
    down.second(3)
    down.third(2)
    ctx = slope.at[:, pl.ds(3 * D, D)]
    grads = slope.at[:, pl.ds(0, 3 * D)]
    dctx = act.at[:, pl.ds(3 * D, D)]
    ctx_load = load(ctx_in, ctx, load_sem.at[0])
    wout_load.wait()

    def context_grad(row, carry):
        rows = pl.ds(pl.multiple_of(row * L, L), L)
        dctx[rows, :] = mm(dab[rows, :], wout[...], NT).astype(BF16)
        return carry

    lax.fori_loop(0, rows_mine, context_grad, 0)
    ctx_load.wait()
    wqkv_load.wait()

    def out_half(core, side):
        cols = pl.ds(pl.multiple_of(384 * side + 128 * core, 128), 256)
        return mm(ctx[...], dab[:, cols], TN)

    def out_parts(side):
        spot = wup.at[:, pl.ds(pl.multiple_of(3 * D + 256 * side, 256), 256)]
        return spot, out.got.at[side].reshape(D, 256)

    def out_other(side, carry):
        out_parts(side)[0][...] = out_half(1 - w.c, side).astype(BF16)
        out.core_copy(side, out_parts).start()
        return carry

    def out_own(side, carry):
        total = out_half(w.c, side).reshape(4, 2, D // 8, 256)
        out.core_wait(side, out.got.at[side])
        out.got[side] = (total + out.got[side].astype(F32)).astype(BF16)
        return carry

    lax.fori_loop(0, 2, out_other, 0)
    lax.fori_loop(0, 2, out_own, 0)
    for step in range(4):
        out.first(step)
    upa.second(0)
    everyone.start()

    qkv = act.at[:, pl.ds(0, 3 * D)]
    qkv_load.wait()
    for copy in lse_load:
        copy.wait()
    x_load.wait()

    def input_grad(row):
        rows = pl.ds(pl.multiple_of(row * L, L), L)
        fb[rows, :] = (mm(grads[rows, :], wqkv[...], NT) + acc[rows, :]).astype(BF16)
        for step in range(3):
            give_back(fb, xgr, xg_sem, row, step).start()
        mine_out(fb, xgr, 1, row).start()

    def qkv_half(core, side, group):
        early = side * 1536 + (1 - side) * core * D
        later = side * (1152 + core * D) + (1 - side) * 384
        start = pl.multiple_of((1 - group) * early + group * later, 128)
        return mm(x[...], grads[:, pl.ds(start, 384)], TN)

    def qkv_sums(group):
        pair = qkv_pair(group)
        start = pl.multiple_of(group * 384, 128)

        def other(turn, carry):
            side = far_first(turn)
            pair_other(pair, side, qkv_half(1 - w.c, side, group), 384, start)
            return carry

        def own(turn, carry):
            side = far_first(turn)
            pair_own(pair, side, turn, qkv_half(w.c, side, group), 384)
            return carry

        lax.fori_loop(0, 2, other, 0)
        lax.fori_loop(0, 2, own, 0)

    def heads_back(i, carry):
        group, row = i // 2, lax.rem(i, 2)
        rows = pl.ds(pl.multiple_of(row * L, L), L)
        keep = r1[rows, pl.ds(pl.multiple_of(group * 128, 128), 128)]
        lanes = [pl.ds(pl.multiple_of(2 * row * 128 + 128 * item, 128), 128) for item in range(2)]
        attend_back(rows, group, 3, qkv, ctx, dctx, keep, grads, feats[:, lanes[0]], feats[:, lanes[1]])

        @pl.when(i == 0)
        def _():
            upa.second(1)
            upb.second(0)
            upb.second(1)
            pair_sent(ups)

        @pl.when(i == 1)
        def _():
            upa.second(2)
            upa.second(3)
            upa.relay()
            upb.second(2)
            down.fourth()

        @pl.when(i == 2)
        def _():
            upb.second(3)
            upb.third(0)
            for step in range(4):
                out.second(step)
            everyone.middle()

        @pl.when(i == 3)
        def _():
            last[0:1, :] = jnp.sum(grads[:, 0:D].astype(F32), axis=0, keepdims=True)
            last[1:2, :] = jnp.sum(grads[:, 2 * D : 3 * D].astype(F32), axis=0, keepdims=True)
            late.start()
            out.relay()
            for step in range(1, 4):
                upb.third(step)
            upa.fourth()

        @pl.when(row == 1)
        def _():
            qkv_sums(group)

        @pl.when(i == 3)
        def _():
            for step in range(4):
                qkvs[0][0].second(step)
            upb.relay()
            out.fourth()
            late.middle()

        @pl.when(group == 1)
        def _():
            input_grad(row)

        @pl.when(i == 2)
        def _():
            for step in range(4):
                qkvs[0][1].second(step)

        return carry

    lax.fori_loop(0, 4, heads_back, 0)
    (qkva, qkvb), (ena, enb) = qkvs
    downo[...] = down.result() * scale
    kept = [load(downo, down_to, mat_sem.at[0])]
    eighth_rows = D // 16
    for step in range(4):
        qkvb.third(step)
    enb.second(0)
    enb.second(1)
    ena.second(0)
    ena.second(1)
    enb.second(2)
    enb.second(3)
    qkva.relay()
    qkvb.relay()
    ena.second(2)
    ena.second(3)
    enb.third(0)
    enb.third(1)
    enb.third(2)
    enb.third(3)
    qkva.fourth()
    upo[eighth_rows:, :] = upb.result() * scale
    ena.fourth()
    outo[...] = pick(out.result() * scale, w.c, 192)
    kept.append(load(outo, out_to, mat_sem.at[1]))
    upo[0:eighth_rows, :] = upa.result() * scale
    kept.append(load(upo, up_to, mat_sem.at[2]))
    vectors = everyone.result() * scale
    vec_out[12:16, :] = jnp.zeros((4, D), F32)
    for index, item in ((3, 7), (5, 2), (6, 0), (7, 1), (8, 3), (9, 4), (10, 5), (11, 6)):
        vec_out[index : index + 1, :] = vectors[item : item + 1, :]
    for index in range(2):
        down.core_copy(2 + index, down_parts).wait_send()
    out.core_sent()
    for total in totals[:4]:
        total.sent()
    everyone.sent()

    def all_sent(source, sem):
        part_sent = source.at[pl.ds(0, 3 * rows_mine * part)]
        remote(part_sent, part_sent, sem, sem, partner(others[0])).wait_send()

    all_sent(ycot, cot_sem.at[0])
    all_sent(ycot, lay_sem.at[0])
    for row in range(rows_mine):
        arrived(lay.at[pl.ds(3 * row, 3)], lay_sem.at[1 + row], partner(others[0]))
        mine_out(ycot, lay, 0, row).wait()
    for group in range(2):
        pair_sent(qkvs[group])
    early = jnp.concatenate([qkva.result(), qkvb.result()], axis=0) * scale
    qkva.sent()
    qkvb.sent()
    ends = late.result() * scale
    vec_out[0:2, :] = ends[0:2, :]
    vec_out[2:3, :] = ends[3:4, :]
    vec_out[4:5, :] = ends[2:3, :]
    kept.append(load(vec_out, vec_to, mat_sem.at[3]))
    late.sent()
    late_part = jnp.concatenate([ena.result(), enb.result()], axis=0) * scale
    for corner, (one, two) in enumerate(
        (
            ((0, 384, 0), (384, 192, 0)), ((192, 384, 0), (0, 192, 192)),
            ((384, 192, 0), (0, 384, 0)), ((0, 192, 192), (192, 384, 0)),
        )
    ):

        @pl.when(w.head == corner)
        def _():
            for value, (place, size, start) in ((early, one), (late_part, two)):
                qkvo[:, place : place + size] = value[:, start : start + size]

    kept.append(load(qkvo, qkv_to, mat_sem.at[4]))
    for row in range(rows_mine):
        arrived(xgr.at[pl.ds(3 * row, 3)], xg_sem.at[1 + row], partner(others[0]))
        mine_out(fb, xgr, 1, row).wait()
    all_sent(fb, xg_sem.at[0])
    ena.sent()
    enb.sent()
    for copy in kept:
        copy.wait()


def pick(values, core, width):
    return jnp.where(core == 0, values[:, :width], values[:, 64 : 64 + width])


VMEM = pl.BlockSpec(memory_space=pltpu.VMEM)
SMEM = pl.BlockSpec(memory_space=pltpu.SMEM)


def shape(dims, kind):
    return jax.ShapeDtypeStruct(dims, kind)


def params(**more):
    return pltpu.CompilerParams(vmem_limit_bytes=255 * 2**18, **more)


def local(
    hidden_in, lengths, qkv_weight, query_bias, value_bias, out_weight, out_bias, gain_one,
    shift_one, up_weight, up_bias, down_weight, down_bias, gain_two, shift_two, cotangent,
):
    row_count, part_len = hidden_in.shape[0], hidden_in.shape[1]
    heads = lax.axis_size("heads")
    mine = row_count // heads
    tokens = mine * L
    ff = up_weight.shape[1]
    place = lax.axis_index("heads")
    x = lax.all_to_all(hidden_in, "heads", split_axis=0, concat_axis=1, tiled=True).reshape(tokens, D)
    cot = lax.all_to_all(cotangent, "heads", split_axis=0, concat_axis=1, tiled=True).reshape(tokens, D)
    lens = lax.dynamic_slice_in_dim(lengths, place * mine, mine, 0)
    bqkv = jnp.concatenate([query_bias, jnp.zeros_like(query_bias), value_bias]).astype(F32)[None]
    qkv, ctx, r1, lse = pl.pallas_call(
        first_kernel,
        out_shape=(
            shape((tokens, 3 * D), BF16), shape((tokens, D), BF16), shape((tokens, D), F32),
            shape((2, tokens, 128), F32),
        ),
        in_specs=[VMEM, SMEM] + [VMEM] * 4,
        out_specs=(VMEM,) * 4,
        scratch_shapes=[pltpu.VMEM((tokens, 128), BF16)] * 2,
        compiler_params=params(),
        name="first",
    )(x, lens, qkv_weight, bqkv, out_weight, out_bias.astype(F32)[None])
    vecs = jnp.stack([gain_one, shift_one, gain_two, shift_two, down_bias]).astype(F32)
    y, dr1, dctx, downg, upg, outg, vec_mid, upb = pl.pallas_call(
        middle_kernel,
        out_shape=(
            shape((tokens, D), BF16), shape((tokens, D), F32), shape((tokens, D), BF16),
            shape((D, ff), BF16), shape((D, ff), BF16), shape((D, D), BF16),
            shape((8, D), F32), shape((1, ff), F32),
        ),
        in_specs=[VMEM] * 8,
        out_specs=(VMEM,) * 8,
        scratch_shapes=[
            pltpu.VMEM((tokens, D), BF16), pltpu.VMEM((tokens, ff), BF16), pltpu.VMEM((tokens, ff), BF16),
            pltpu.VMEM((tokens, D), F32), pltpu.VMEM((tokens, D), BF16), pltpu.VMEM((tokens, D), BF16),
        ],
        compiler_params=params(),
        name="middle",
    )(r1, ctx, cot, vecs, up_weight, up_bias.astype(F32)[None], down_weight, out_weight)
    xg, qkvg, vec_last = pl.pallas_call(
        last_kernel,
        out_shape=(shape((tokens, D), BF16), shape((D, 3 * D), BF16), shape((8, D), F32)),
        in_specs=[VMEM, SMEM] + [VMEM] * 6,
        out_specs=(VMEM,) * 3,
        scratch_shapes=[pltpu.VMEM((tokens, 3 * D), BF16)] + [pltpu.VMEM((tokens, 128), BF16)] * 2,
        compiler_params=params(),
        name="last",
    )(x, lens, qkv, ctx, dctx, lse, dr1, qkv_weight)

    def back(values):
        values = values.reshape(mine, L, D)
        return lax.all_to_all(values, "heads", split_axis=1, concat_axis=0, tiled=True)

    layer_out = back(y)
    input_grad = back(xg).astype(F32)
    scale = 1.0 / (row_count * lax.axis_size("rows"))
    vec_mid, vec_last, upb = lax.psum((vec_mid, vec_last, upb), ("rows", "heads"))

    def reduce(values, flip):
        one, two = (0, 1) if flip else (1, 0)
        half = lax.psum_scatter(values, "heads", scatter_dimension=one, tiled=True).astype(F32)
        total = lax.psum_scatter(half, "rows", scatter_dimension=two, tiled=True) * scale
        return total.T if flip else total

    vm, vl = vec_mid * scale, vec_last * scale
    return (
        layer_out, input_grad, reduce(qkvg, False), vl[0], vl[1], reduce(outg, False), vm[5], vm[3], vm[4],
        reduce(upg, False), upb[0] * scale, reduce(downg, True), vm[2], vm[0], vm[1],
    )


ANY = pl.BlockSpec(memory_space=pl.ANY)
DMA = pltpu.SemaphoreType.DMA
BLOCKS = (("yzx", 192, 384, 4), ("yzx", 48, 768, 2), ("xyz", 48, 768, 2), ("yzx", 96, 256, 2))
JOINT = (("yZx", 48, 384, 2), ("xyZ", 48, 384, 2))


def finish_kernel(count, *refs):
    lay, xgr, vec = refs[:3]
    mats = refs[3 : 3 + count]
    lay_out, xg_out = refs[3 + count : 5 + count]
    mats_out = refs[5 + count : 5 + 2 * count]
    vecs_out = refs[5 + 2 * count : 14 + 2 * count]
    through, low, full, sems = refs[14 + 2 * count : 18 + 2 * count]
    mats_here, (vec_here, mat_sems) = refs[18 + 2 * count : 18 + 3 * count], refs[-2:]
    vec_load = load(vec, vec_here, mat_sems.at[0, count])
    blocks = xgr.shape[0]
    wides = [load(xgr.at[i], low.at[i], sems.at[0, i]) for i in range(blocks)]
    lays = [load(lay.at[i], through.at[i], sems.at[1, i]) for i in range(blocks)]
    arrive = [load(mats[i], mats_here[i], mat_sems.at[0, i]) for i in range(count)]
    copies = []
    for i in range(blocks):
        wides[i].wait()
        full[i] = low[i].astype(F32)
        copies.append(load(full.at[i], xg_out.at[i], sems.at[2, i]))
    for i in range(blocks):
        lays[i].wait()
        copies.append(load(through.at[i], lay_out.at[i], sems.at[3, i]))
    for i in range(count):
        arrive[i].wait()
        copies.append(load(mats_here[i], mats_out[i], mat_sems.at[1, i]))
    vec_load.wait()
    for index in range(8):
        vecs_out[index][...] = vec_here[index, :]
    for index in range(4):
        vecs_out[8][index * D : (index + 1) * D] = vec_here[8 + index, :]
    for copy in copies:
        copy.wait()


def local_fast(
    hidden_in, lengths, qkv_weight, query_bias, value_bias, out_weight, out_bias, gain_one,
    shift_one, up_weight, up_bias, down_weight, down_bias, gain_two, shift_two, cotangent,
):
    row_count, part_len = hidden_in.shape[0], hidden_in.shape[1]
    mine = row_count // lax.axis_size("heads")
    heads = lax.axis_size("heads")
    tokens = mine * L
    ff = up_weight.shape[1]
    bf = lambda *dims: pltpu.VMEM(dims, BF16)
    fl = lambda *dims: pltpu.VMEM(dims, F32)
    x, qkv, ctx, r1, lse = pl.pallas_call(
        gather_kernel,
        out_shape=(
            shape((tokens, D), BF16), shape((tokens, 3 * D), BF16),
            shape((tokens, D), BF16), shape((tokens, D), F32), shape((2, tokens, 128), F32),
        ),
        in_specs=[ANY, VMEM, ANY, VMEM, VMEM, ANY, VMEM],
        out_specs=(ANY,) * 5,
        scratch_shapes=[
            bf(tokens, D), bf(tokens, 3 * D), bf(tokens, D), fl(tokens, D), fl(2, tokens, 128), bf(D, 3 * D),
            bf(D, D), fl(8, D), bf(tokens, 128), bf(tokens, 128),
            DMA((2,)), DMA((mine,)), DMA((5, mine)), DMA((mine, heads - 1)), DMA((mine, heads)),
        ],
        compiler_params=params(collective_id=0, has_side_effects=True),
        name="gather",
    )(hidden_in, lengths.T, qkv_weight, query_bias, value_bias, out_weight, out_bias)
    scale = 1.0 / (row_count * lax.axis_size("rows"))
    totals = []
    for block in BLOCKS:
        totals += Total.scratch(*block)
    for block in JOINT:
        totals += Total.scratch(*block, groups=(2,))
    mats = (shape((192, 384), F32), shape((96, 768), F32), shape((96, 192), F32), shape((96, 576), F32))
    wide_out = shape((row_count, part_len, D), BF16)
    lay, xgr, downg, upg, outg, qkvg, vec = pl.pallas_call(
        functools.partial(rest_kernel, scale),
        out_shape=(wide_out, wide_out) + mats + (shape((16, D), F32),),
        in_specs=[ANY] * 6 + [VMEM] + [ANY] * 4 + [VMEM] * 6,
        out_specs=(ANY,) * 7,
        scratch_shapes=[fl(*item.shape) for item in mats] + [
            fl(16, D), DMA((5,)),
            fl(tokens, D), bf(tokens, D), bf(tokens, D), bf(tokens, ff), bf(tokens, ff),
            fl(tokens, D), bf(tokens, D), bf(4, D // 4, tokens), bf(D, ff), bf(ff, D),
            bf(2, 2, 2, 192, 384), DMA((13,)), DMA((1 + mine,)), DMA((1 + mine,)), DMA((1 + mine,)), DMA((3, mine)),
        ]
        + totals
        + Everyone.scratch(8)
        + Everyone.scratch(8),
        compiler_params=params(collective_id=1, has_side_effects=True),
        name="rest",
    )(
        r1, cotangent, ctx, qkv, lse, x, lengths.T, up_weight, down_weight, out_weight, qkv_weight,
        gain_one, shift_one, gain_two, shift_two, down_bias, up_bias,
    )
    results = pl.pallas_call(
        functools.partial(finish_kernel, 4),
        out_shape=(wide_out, shape((row_count, part_len, D), F32)) + mats + (shape((D,), F32),) * 8 + (shape((ff,), F32),),
        in_specs=[ANY] * 7,
        out_specs=(ANY,) * 6 + (VMEM,) * 9,
        scratch_shapes=[
            bf(row_count, part_len, D), bf(row_count, part_len, D), fl(row_count, part_len, D), DMA((4, row_count)),
        ]
        + [fl(*item.shape) for item in mats]
        + [fl(16, D), DMA((2, 5))],
        compiler_params=params(),
        name="finish",
    )(lay, xgr, vec, downg, upg, outg, qkvg)
    layer_out, input_grad, downg, upg, outg, qkvg, qb, vb, ob, go, so, db, gt, st, ub = results
    return layer_out, input_grad, qkvg, qb, vb, outg, ob, go, so, upg, ub, downg.T, db, gt, st


def solution(mesh):
    split = P("rows", "heads", None)
    grid = P("rows", "heads")
    in_specs = (split, P("rows", None)) + (P(),) * 13 + (split,)
    out_specs = (split, split, grid, P(), P(), grid, P(), P(), P(), grid, P(), grid, P(), P(), P())
    fast = mesh.shape["rows"] == 8 and mesh.shape["heads"] == 4
    return jax.shard_map(
        local_fast if fast else local, mesh=mesh, in_specs=in_specs, out_specs=out_specs, check_vma=False
    )
```

profile of v0, /device:TPU:0, one launch (start us, length us, event | category | flops | bytes accessed | tf_op | source)
XLA Modules:
  0.0 166.3 jit_solution(11059165060907078416)
XLA Ops:
  0.6 26.2 %gather.1 = (bf16[1024,768]{1,0:T(8,128)(2,1)}, bf16[1024,2304]{1,0:T(8,128)(2,1)}, bf16[1024,768]{1,0:T(8,128)(2,1)}, f32[1024,768]{1,0:T(8,128)}, f32[2,1024,128]{2,1,0:T(8,128)}) custom-call(bf16[8,128,768]{2,1,0:T(8,128)(2,1)} %hidden.1, s32[4,8]{1,0:T(4,128)} %bitcast.2, bf16[768,2304]{1,0:T(8,128)(2,1)} %wqkv_in.3, bf16[768]{0:T(1024)(128)(2,1)} %bq.1, ...), custom_call_target="tpu_custom_call" | custom-call | tf_op jit(solution)/shard_map/gather/pallas_call | solution.py:1350
  26.8 134.4 %rest.1 = (bf16[8,128,768]{2,1,0:T(8,128)(2,1)}, bf16[8,128,768]{2,1,0:T(8,128)(2,1)}, f32[192,384]{1,0:T(8,128)}, f32[96,768]{1,0:T(8,128)}, f32[96,192]{1,0:T(...) custom-call(f32[1024,768]{1,0:T(8,128)} %get-tuple-element.42.r1_in, bf16[8,128,768]{2,1,0:T(8,128)(2,1)} %cotan.1, ...), custom_call_target="tpu_custom_call" | custom-call | tf_op jit(solution)/shard_map/rest/pallas_call | solution.py:1374
  161.2 4.9 %finish.1 = (bf16[8,128,768]{2,1,0:T(8,128)(2,1)}, f32[8,128,768]{2,1,0:T(8,128)}, f32[192,384]{1,0:T(8,128)}, f32[96,768]{1,0:T(8,128)}, f32[96,192]{1,0:T(8,12...) custom-call(bf16[8,128,768]{2,1,0:T(8,128)(2,1)} %get-tuple-element., ...), custom_call_target="tpu_custom_call" | custom-call | tf_op jit(solution)/shard_map/finish/pallas_call | solution.py:1394
where the time goes:
time: 167 us; the launch traced here: 166 us
  Pallas kernels  165 us (99%)
    pallas_call x1, Pallas kernels, local_fast(): pl.pallas_call(functools.partial(rest_kernel, scale), out_shape=(wide_out...  134 us
    pallas_call x1, Pallas kernels, local_fast(): pl.pallas_call(gather_kernel, out_shape=(shape((tokens, D), BF16), shape(...  26.2 us
    pallas_call x1, Pallas kernels, local_fast(): pl.pallas_call(functools.partial(finish_kernel, 4), out_shape=(wide_out,...  4.89 us

commit v1 on v0

--- a/solution.py
+++ b/solution.py
@@ -933,24 +933,30 @@
 
     ups = (upa, upb)
 
-    def spot(side, index, cols, start):
-        row = pl.multiple_of(side * D + index * (D // 2), D // 2)
-        return wdown.at[pl.ds(row, D // 2), pl.ds(start, cols)]
-
-    def pair_parts(each, index, cols, start):
-        return lambda side: (spot(side, index, cols, start), each.got.at[side].reshape(D // 2, cols))
-
-    def pair_other(pair, side, total, cols, start):
-        total = total.astype(BF16).reshape(4, 2, 2, D // 16, cols)
-        for index, each in enumerate(pair):
-            spot(side, index, cols, start)[...] = total[:, :, index].reshape(D // 2, cols)
-            each.core_copy(side, pair_parts(each, index, cols, start)).start()
-
-    def pair_own(pair, side, turn, total, cols):
-        total = total.reshape(4, 2, 2, D // 16, cols)
-        for index, each in enumerate(pair):
+    def spot(side, index, pair, start):
+        rows, cols = pair[index].got.shape[-2:]
+        row = pl.multiple_of(side * D + index * (D - 8 * rows), 128)
+        return wdown.at[pl.ds(row, 8 * rows), pl.ds(start, cols)], each_got(pair[index], side)
+
+    def each_got(each, side):
+        rows, cols = each.got.shape[-2:]
+        return each.got.at[side].reshape(8 * rows, cols)
+
+    def pair_rows(pair, total):
+        edge, cols = pair[0].got.shape[-2:]
+        total = total.reshape(4, 2, D // 8, cols)
+        return total[:, :, :edge], total[:, :, edge:]
+
+    def pair_other(pair, side, total, start):
+        for index, rows in enumerate(pair_rows(pair, total.astype(BF16))):
+            place, target = spot(side, index, pair, start)
+            place[...] = rows.reshape(place.shape)
+            pair[index].core_copy(side, lambda _: (place, target)).start()
+
+    def pair_own(pair, side, turn, total):
+        for each, rows in zip(pair, pair_rows(pair, total)):
             each.core_wait(side, each.got.at[side])
-            each.got[side] = (total[:, :, index] + each.got[side].astype(F32)).astype(BF16)
+            each.got[side] = (rows + each.got[side].astype(F32)).astype(BF16)
         for when, each in enumerate((pair[1], pair[0])):
 
             @pl.when(turn == when)
@@ -967,7 +973,7 @@
 
     def up_other(turn, carry):
         side = far_first(turn)
-        pair_other(ups, side, up_half(1 - w.c, side), width, 0)
+        pair_other(ups, side, up_half(1 - w.c, side), 0)
         return carry
 
     lax.fori_loop(0, 2, up_other, 0)
@@ -977,7 +983,7 @@
 
     def up_own(turn, carry):
         side = far_first(turn)
-        pair_own(ups, side, turn, up_half(w.c, side), width)
+        pair_own(ups, side, turn, up_half(w.c, side))
         return carry
 
     lax.fori_loop(0, 2, up_own, 0)
@@ -1049,12 +1055,12 @@
 
         def other(turn, carry):
             side = far_first(turn)
-            pair_other(pair, side, qkv_half(1 - w.c, side, group), 384, start)
+            pair_other(pair, side, qkv_half(1 - w.c, side, group), start)
             return carry
 
         def own(turn, carry):
             side = far_first(turn)
-            pair_own(pair, side, turn, qkv_half(w.c, side, group), 384)
+            pair_own(pair, side, turn, qkv_half(w.c, side, group))
             return carry
 
         lax.fori_loop(0, 2, other, 0)
@@ -1127,7 +1133,7 @@
     (qkva, qkvb), (ena, enb) = qkvs
     downo[...] = down.result() * scale
     kept = [load(downo, down_to, mat_sem.at[0])]
-    eighth_rows = D // 16
+    edge = upa.got.shape[-2]
     for step in range(4):
         qkvb.third(step)
     enb.second(0)
@@ -1145,11 +1151,11 @@
     enb.third(2)
     enb.third(3)
     qkva.fourth()
-    upo[eighth_rows:, :] = upb.result() * scale
+    upo[edge:, :] = upb.result() * scale
     ena.fourth()
     outo[...] = pick(out.result() * scale, w.c, 192)
     kept.append(load(outo, out_to, mat_sem.at[1]))
-    upo[0:eighth_rows, :] = upa.result() * scale
+    upo[0:edge, :] = upa.result() * scale
     kept.append(load(upo, up_to, mat_sem.at[2]))
     vectors = everyone.result() * scale
     vec_out[12:16, :] = jnp.zeros((4, D), F32)
@@ -1300,7 +1306,7 @@
 ANY = pl.BlockSpec(memory_space=pl.ANY)
 DMA = pltpu.SemaphoreType.DMA
 BLOCKS = (("yzx", 192, 384, 4), ("yzx", 48, 768, 2), ("xyz", 48, 768, 2), ("yzx", 96, 256, 2))
-JOINT = (("yZx", 48, 384, 2), ("xyZ", 48, 384, 2))
+JOINT = (("yZx", 32, 384, 2), ("xyZ", 64, 384, 2))
 
 
 def finish_kernel(count, *refs):

time: 167 us -> 165 us (0.988)
  no operation moved by 1% of the time
where the time goes in v1:
time: 165 us
  Pallas kernels  164 us (99%)
    pallas_call x1, Pallas kernels, local_fast(): pl.pallas_call(functools.partial(rest_kernel, scale), out_shape=(wide_out...  133 us
    pallas_call x1, Pallas kernels, local_fast(): pl.pallas_call(gather_kernel, out_shape=(shape((tokens, D), BF16), shape(...  26.2 us
    pallas_call x1, Pallas kernels, local_fast(): pl.pallas_call(functools.partial(finish_kernel, 4), out_shape=(wide_out,...  4.89 us

profile of v1, /device:TPU:0, one launch (start us, length us, event | category | flops | bytes accessed | tf_op | source)
XLA Modules:
  0.0 165.1 jit_solution(8045229743510470640)
XLA Ops:
  0.6 26.2 %gather.1 = (bf16[1024,768]{1,0:T(8,128)(2,1)}, bf16[1024,2304]{1,0:T(8,128)(2,1)}, bf16[1024,768]{1,0:T(8,128)(2,1)}, f32[1024,768]{1,0:T(8,128)}, f32[2,1024,128]{2,1,0:T(8,128)}) custom-call(bf16[8,128,768]{2,1,0:T(8,128)(2,1)} %hidden.1, s32[4,8]{1,0:T(4,128)} %bitcast.2, bf16[768,2304]{1,0:T(8,128)(2,1)} %wqkv_in.3, bf16[768]{0:T(1024)(128)(2,1)} %bq.1, ...), custom_call_target="tpu_custom_call" | custom-call | tf_op jit(solution)/shard_map/gather/pallas_call | solution.py:1356
  26.8 133.2 %rest.1 = (bf16[8,128,768]{2,1,0:T(8,128)(2,1)}, bf16[8,128,768]{2,1,0:T(8,128)(2,1)}, f32[192,384]{1,0:T(8,128)}, f32[96,768]{1,0:T(8,128)}, f32[96,192]{1,0:T(...) custom-call(f32[1024,768]{1,0:T(8,128)} %get-tuple-element.42.r1_in, bf16[8,128,768]{2,1,0:T(8,128)(2,1)} %cotan.1, ...), custom_call_target="tpu_custom_call" | custom-call | tf_op jit(solution)/shard_map/rest/pallas_call | solution.py:1380
  160.0 4.9 %finish.1 = (bf16[8,128,768]{2,1,0:T(8,128)(2,1)}, f32[8,128,768]{2,1,0:T(8,128)}, f32[192,384]{1,0:T(8,128)}, f32[96,768]{1,0:T(8,128)}, f32[96,192]{1,0:T(8,12...) custom-call(bf16[8,128,768]{2,1,0:T(8,128)(2,1)} %get-tuple-element., ...), custom_call_target="tpu_custom_call" | custom-call | tf_op jit(solution)/shard_map/finish/pallas_call | solution.py:1400
